TPU v7x, 256 devices: a whole 4x4x8 slice. The times are simulated.
256 devices in a mesh: row: 16 (over x, z_hi), col: 16 (over y, z_lo, core).
Axes of the slice: x: 4, y: 4, z: 8 (z_hi: 4, z_lo: 2; z = z_hi * 2 + z_lo), core: 2. Of those that a mesh axis runs over, the one named last changes fastest.
Arguments:
- amplitudes: bfloat16 [1280, 32768], P('row', 'col'), may hold values from -6 to 6
- integrals: bfloat16 [32768, 16384], P('col', 'row'), may hold values from -0.046875 to 0.046875
Outputs:
- ladder: bfloat16 [16384, 1280], P(('row', 'col'))
All inputs are finite; a program needn't handle non-finite values.
Results may differ from a plain program's by a relative error of at most 0.001.
Values may be sent and summed in bfloat16 or wider, within the bound.
No kernel may reach another device: no remote copies, remote signals or barrier semaphores. Data moves between devices by JAX's collectives and lax.ppermute only.
A program may use at most 64 MiB of HBM per device.

v0:
```python
import jax
import jax.numpy as jnp
from jax import lax
from jax.sharding import PartitionSpec as P


def local(amplitudes, integrals):
    partial_value = jnp.dot(
        lax.all_gather(amplitudes, "row", axis=0, tiled=True),
        integrals,
        preferred_element_type=jnp.float32,
    )
    summed = lax.psum_scatter(partial_value, "col", scatter_dimension=0, tiled=True)
    turned = summed.astype(jnp.bfloat16).T
    return lax.all_to_all(turned, "col", split_axis=0, concat_axis=1, tiled=True)


def solution(mesh):
    placed = (P("row", "col"), P("col", "row"))
    return jax.shard_map(
        local, mesh=mesh, in_specs=placed, out_specs=P(("row", "col"), None), check_vma=False
    )
```

profile of v0, /device:TPU:1, one launch (start us, length us, event | category | flops | bytes accessed | tf_op | source)
XLA Modules:
  0.0 205.7 jit_solution(17190738923694836563)
XLA Ops:
  6.5 0.0 all-gather.2.cloned.1.call-start
  6.5 0.7 all-gather.2.cloned.1.call-update
  7.3 0.0 reduce-scatter.2.cloned.1.call-start
  7.3 94.3 %all-gather.2.cloned.1.call-done = bf16[1280,2048]{1,0:T(8,128)(2,1)} async-done(((bf16[80,2048]{1,0:T(8,128)(2,1)}), bf16[1280,2048]{1,0:T(8,128)(2,1)}) %all-gather.2.cloned.1.call-update) | async-done | bytes 5242896 | tf_op jit(solution)/shard_map/all_gather | solution.py:9
  101.6 10.2 %fusion = f32[1280,1024]{1,0:T(8,128)} fusion(bf16[1280,2048]{1,0:T(8,128)(2,1)} %all-gather.2.cloned.1.call-done, bf16[2048,1024]{1,0:T(8,128)(2,1)} %param.3), kind=kOutput, calls=%fused_computation.1 | convolution fusion | flops 5368709120 | bytes 14680064 | tf_op jit(solution)/shard_map/dot_general | solution.py:8
  111.9 0.0 reduce-scatter.2.cloned.1.call-update
  111.9 71.5 %reduce-scatter.2.cloned.1.call-done = f32[80,1024]{1,0:T(8,128)} async-done(((f32[1280,1024]{1,0:T(8,128)}), f32[80,1024]{1,0:T(8,128)}) %reduce-scatter.2.cloned.1.call-update) | async-done | bytes 327696 | tf_op jit(solution)/shard_map/reduce_scatter | solution.py:13
  183.5 1.0 convert_bitcast_fusion
  184.4 0.2 copy.7
  184.6 13.1 %all_to_all.19 = bf16[16,64,80]{2,1,0:T(8,128)(2,1)S(1)} all-to-all(bf16[16,64,80]{2,1,0:T(8,128)(2,1)S(1)} %bitcast.7), channel_id=1, replica_groups=mesh['row'=16,'col'=16] {'col'}, dimensions={0} | all-to-all | bytes 327680 | tf_op jit(solution)/shard_map/all_to_all | solution.py:15
  197.8 0.2 copy.6
  197.9 0.9 all_to_all.17
Async XLA Ops:
  6.5 95.1 %all-gather.2.cloned.1.call-start = ((), (), s32[]{:S(2)}) async-start(), calls=%async_computation.2 | async-start | bytes 5570560 | tf_op jit(solution)/shard_map/all_gather | solution.py:9
  7.3 176.2 %reduce-scatter.2.cloned.1.call-start = ((), (), s32[]{:S(2)}) async-start(), calls=%async_computation.3 | async-start | bytes 5570560 | tf_op jit(solution)/shard_map/reduce_scatter | solution.py:13
Sparse Core Ops, SparseCore 0:
  9.8 91.7 all-gather.1
  112.0 71.3 reduce-scatter.1
where the time goes:
time: 206 us
  waiting for transfers between devices  167 us (81%)
  between operations  13.4 us (7%)
  blocking collectives  13.1 us (6%)
  matrix products  10.2 us (5%)
    all_gather x1, waiting for transfers between devices, local(): lax.all_gather(amplitudes, 'row', axis=0, tiled=True)  94.3 us
    reduce_scatter x1, waiting for transfers between devices, local(): lax.psum_scatter(partial_value, 'col', scatter_dimension=0, tiled=True)  71.5 us
    all_to_all x1, blocking collectives, local(): lax.all_to_all(turned, 'col', split_axis=0, concat_axis=1, tiled=True)  13.1 us
    dot_general x1, matrix products, local(): jnp.dot(lax.all_gather(amplitudes, 'row', axis=0, tiled=True), integrals,...  10.2 us
  transfers between devices with their start and end apart: 2, of which 2 were waited for; matrix products, arithmetic and copies ran while one was open for 0% of the time, Pallas kernels for 0%

commit v1 on v0

--- a/solution.py
+++ b/solution.py
@@ -6,7 +6,9 @@
 
 def local(amplitudes, integrals):
     partial_value = jnp.dot(
-        lax.all_gather(amplitudes, "row", axis=0, tiled=True),
+        jnp.concatenate(
+            lax.all_to_all(jnp.stack([amplitudes] * lax.axis_size("row")), "row", 0, 0), axis=0
+        ),
         integrals,
         preferred_element_type=jnp.float32,
     )

time: 206 us -> 239 us (1.16)
  blocking collectives: 13.1 us -> 141 us
  waiting for transfers between devices: 167 us -> 72.4 us
  matrix products: 10.2 us -> 7.35 us
    all_to_all x0 -> x1, blocking collectives: none -> 128 us  [local(): lax.all_to_all(jnp.stack([amplitudes] * lax.axis_size('row')), 'row', 0, 0)]
    all_gather x1 -> x0, waiting for transfers between devices: 94.3 us -> none  [local(): lax.all_gather(amplitudes, 'row', axis=0, tiled=True)]
    dot_general x1, matrix products: 10.2 us -> 7.35 us  [local(): jnp.dot(jnp.concatenate(lax.all_to_all(jnp.stack([amplitudes] * lax.axis_...]
  transfers between devices with their start and end apart: 2 -> 1, of which waited for: 2 -> 1; matrix products, arithmetic and copies ran while one was open for 0% -> 0% of each run, Pallas kernels for 0% -> 0%
where the time goes in v1:
time: 239 us; the launch traced here: 238 us
  blocking collectives  141 us (59%)
  waiting for transfers between devices  72.4 us (30%)
  between operations  13.4 us (6%)
  matrix products  7.35 us (3%)
  local copies, waits for them, and re-layouts  2.9 us (1%)
    all_to_all x1, blocking collectives, local(): lax.all_to_all(jnp.stack([amplitudes] * lax.axis_size('row')), 'row', 0, 0)  128 us
    reduce_scatter x1, waiting for transfers between devices, local(): lax.psum_scatter(partial_value, 'col', scatter_dimension=0, tiled=True)  72.4 us
    all_to_all x1, blocking collectives, local(): lax.all_to_all(turned, 'col', split_axis=0, concat_axis=1, tiled=True)  13.1 us
    dot_general x1, matrix products, local(): jnp.dot(jnp.concatenate(lax.all_to_all(jnp.stack([amplitudes] * lax.axis_...  7.35 us
  transfers between devices with their start and end apart: 1, of which 1 were waited for; matrix products, arithmetic and copies ran while one was open for 0% of the time, Pallas kernels for 0%

profile of v1, /device:TPU:1, one launch (start us, length us, event | category | flops | bytes accessed | tf_op | source)
XLA Modules:
  0.0 238.4 jit_solution(12850287902368599128)
XLA Ops:
  6.5 0.0 reduce-scatter.2.cloned.1.call-start
  6.5 1.6 stack.2
  8.2 0.0 copy-start
  8.2 128.1 %all_to_all.24 = bf16[16,80,2048]{2,1,0:T(8,128)(2,1)S(1)} all-to-all(bf16[16,80,2048]{2,1,0:T(8,128)(2,1)S(1)} %stack.2), channel_id=1, replica_groups=mesh['row'=16,'col'=16] {'row'}, dimensions={0} | all-to-all | bytes 10485760 | tf_op jit(solution)/shard_map/all_to_all | solution.py:10
  136.3 0.0 copy-done
  136.3 7.3 %fusion = f32[1280,1024]{1,0:T(8,128)} fusion(bf16[1280,2048]{1,0:T(8,128)(2,1)S(1)} %bitcast.7, bf16[2048,1024]{1,0:T(8,128)(2,1)S(1)} %copy-done), kind=kOutput, calls=%fused_computation.1 | convolution fusion | flops 5368709120 | bytes 14680064 | tf_op jit(solution)/shard_map/dot_general | solution.py:8
  143.7 0.0 reduce-scatter.2.cloned.1.call-update
  143.7 72.4 %reduce-scatter.2.cloned.1.call-done = f32[80,1024]{1,0:T(8,128)} async-done(((f32[1280,1024]{1,0:T(8,128)}), f32[80,1024]{1,0:T(8,128)}) %reduce-scatter.2.cloned.1.call-update) | async-done | bytes 327696 | tf_op jit(solution)/shard_map/reduce_scatter | solution.py:15
  216.1 1.0 convert_bitcast_fusion
  217.1 0.2 copy.7
  217.3 13.1 %all_to_all.25 = bf16[16,64,80]{2,1,0:T(8,128)(2,1)S(1)} all-to-all(bf16[16,64,80]{2,1,0:T(8,128)(2,1)S(1)} %bitcast.9), channel_id=1, replica_groups=mesh['row'=16,'col'=16] {'col'}, dimensions={0} | all-to-all | bytes 327680 | tf_op jit(solution)/shard_map/all_to_all | solution.py:17
  230.4 0.2 copy.6
  230.6 0.9 all_to_all.21
Async XLA Ops:
  6.5 209.6 %reduce-scatter.2.cloned.1.call-start = ((), (), s32[]{:S(2)}) async-start(), calls=%async_computation.3 | async-start | bytes 5570560 | tf_op jit(solution)/shard_map/reduce_scatter | solution.py:15
  8.2 128.2 %copy-start = (bf16[2048,1024]{1,0:T(8,128)(2,1)S(1)}, bf16[2048,1024]{1,0:T(8,128)(2,1)}, u32[]{:S(2)}) copy-start(bf16[2048,1024]{1,0:T(8,128)(2,1)} %param.3) | copy-start | bytes 12582916
Sparse Core Ops, SparseCore 0:
  143.8 72.2 reduce-scatter.1
